TPU v7x, 512 devices: a whole 4x4x16 slice. The times are simulated.
512 devices in a mesh: seq: 32 (over x, y, z_hi), head: 16 (over z_lo, core).
Axes of the slice: x: 4, y: 4, z: 16 (z_hi: 2, z_lo: 8; z = z_hi * 8 + z_lo), core: 2. Of those that a mesh axis runs over, the one named last changes fastest.
Arguments:
- query_rows: bfloat16 [16384, 4096], P('seq', 'head'), may hold values from -100 to 100
- key_rows: bfloat16 [16384, 4096], P('seq', 'head'), may hold values from -4 to 4
- value_rows: bfloat16 [16384, 4096], P('seq', 'head'), may hold values from -6 to 6
- out_grad: bfloat16 [16384, 4096], P('seq', 'head'), may hold values from -6 to 6
- members: int32 [16384], P(('seq', 'head')), may hold values from 0 to 16383, as said below
Outputs:
- attn_out: bfloat16 [16384, 4096], P('seq', 'head')
- query_grad: bfloat16 [16384, 4096], P('seq', 'head')
- key_grad: bfloat16 [16384, 4096], P('seq', 'head')
- value_grad: bfloat16 [16384, 4096], P('seq', 'head')
Inputs may be any that keep to these rules, and one draw needn't show every extreme that they name: `members`: every position appears once; the 512 positions of each cluster stand in ascending order. Of the 512 positions of one index of seq a cluster takes 0, 16 or 32, and for each index of seq some clusters take 32. The positions may be sent packed, several to a 32-bit word, or in any narrower integer form that holds them exactly.
All inputs are finite; a program needn't handle non-finite values.
Results may differ from a plain program's by a relative error of at most 0.008.
Values may be sent and summed in bfloat16 or wider, within the bound.
A program may use at most 64 MiB of HBM per device.

v0:
```python
import math

import jax
import jax.numpy as jnp
from jax import lax
from jax.sharding import PartitionSpec as P

CLUS = 512
WINDOW = 512


def from_behind(array, axis, by):
    count = lax.axis_size(axis)
    pairs = [(i, i + by) for i in range(count) if 0 <= i + by < count]
    return lax.ppermute(array, axis, pairs)


def attend(query_matrix, input_keys, value_matrix, upstream_gradient, allowed, backward):
    logit_scale = 1.0 / math.sqrt(query_matrix.shape[-1])
    attention_scores = (
        jnp.einsum("vnw,vtw->vnt", query_matrix, input_keys, preferred_element_type=jnp.float32)
        * logit_scale
    )
    attention_scores = jnp.where(allowed, attention_scores, -jnp.inf)
    row_max = jnp.max(attention_scores, axis=-1, keepdims=True)
    exp_scores = jnp.exp(attention_scores - row_max)
    probability = exp_scores / jnp.sum(exp_scores, axis=-1, keepdims=True)
    attention_weights = probability.astype(jnp.bfloat16)
    attended_output = jnp.einsum(
        "yxs,ysl->yxl", attention_weights, value_matrix, preferred_element_type=jnp.float32
    )
    if not backward:
        return (attended_output,)
    probability_gradient = jnp.einsum(
        "vnw,vtw->vnt", upstream_gradient, value_matrix, preferred_element_type=jnp.float32
    )
    row_delta = jnp.sum(probability * probability_gradient, axis=-1, keepdims=True)
    score_gradient = (probability * (probability_gradient - row_delta) * logit_scale).astype(
        jnp.bfloat16
    )
    query_gradient = jnp.einsum(
        "yxs,ysl->yxl", score_gradient, input_keys, preferred_element_type=jnp.float32
    )
    key_gradient = jnp.einsum(
        "ipy,ipg->iyg", score_gradient, query_matrix, preferred_element_type=jnp.float32
    )
    value_gradient = jnp.einsum(
        "ipy,ipg->iyg", attention_weights, upstream_gradient, preferred_element_type=jnp.float32
    )
    return (attended_output, query_gradient, key_gradient, value_gradient)


def window_head(query_matrix, input_keys, value_matrix, upstream_gradient):
    tok_rows = query_matrix.shape[0]
    window_len = WINDOW
    blocks = tok_rows // window_len
    rim_keys, rim_values = from_behind((input_keys, value_matrix), "seq", 1)
    extended_keys = jnp.concatenate([rim_keys, input_keys], axis=0)
    extended_values = jnp.concatenate([rim_values, value_matrix], axis=0)

    def framed(extended):
        return jnp.concatenate(
            [
                extended[:tok_rows].reshape(blocks, window_len, -1),
                extended[window_len:].reshape(blocks, window_len, -1),
            ],
            axis=1,
        )

    def unframe(blockwise):
        lower_half = blockwise[:, :window_len].reshape(tok_rows, -1)
        upper_half = blockwise[:, window_len:].reshape(tok_rows, -1)
        return jnp.pad(lower_half, ((0, window_len), (0, 0))) + jnp.pad(
            upper_half, ((window_len, 0), (0, 0))
        )

    offset = lax.axis_index("seq") * tok_rows
    query_pos = jnp.arange(window_len)[None, :, None]
    key_pos = jnp.arange(2 * window_len)[None, None, :]
    block_pos = jnp.arange(blocks)[:, None, None]
    allowed = (
        (key_pos > query_pos)
        & (key_pos <= query_pos + window_len)
        & (offset + block_pos * window_len + key_pos >= window_len)
    )
    attended_output, query_gradient, key_gradient, value_gradient = attend(
        query_matrix.reshape(blocks, window_len, -1),
        framed(extended_keys),
        framed(extended_values),
        upstream_gradient.reshape(blocks, window_len, -1),
        allowed,
        True,
    )
    full_keys = unframe(key_gradient)
    full_values = unframe(value_gradient)
    later_keys, later_values = (
        from_behind(full_keys[:window_len].astype(jnp.bfloat16), "seq", -1).astype(jnp.float32),
        from_behind(full_values[:window_len].astype(jnp.bfloat16), "seq", -1).astype(jnp.float32),
    )
    own_keys = full_keys[window_len:].at[tok_rows - window_len :].add(later_keys)
    own_values = full_values[window_len:].at[tok_rows - window_len :].add(later_values)
    return (
        attended_output.reshape(tok_rows, -1).astype(jnp.bfloat16),
        query_gradient.reshape(tok_rows, -1).astype(jnp.bfloat16),
        own_keys.astype(jnp.bfloat16),
        own_values.astype(jnp.bfloat16),
    )


def on_device(query_rows, key_rows, value_rows, out_grad, members):
    tok_rows = query_rows.shape[0]
    head_dim = query_rows.shape[1] // 2
    all_members = lax.all_gather(members, ("seq", "head"), axis=0, tiled=True)
    shards = lax.axis_size("seq")
    me_index = lax.axis_index("seq")
    clusters = all_members.shape[0] // CLUS
    per_dev = clusters // shards
    capacity = 2 * (CLUS // shards)
    total = clusters * capacity
    member_table = all_members.reshape(clusters, CLUS)
    source = member_table // tok_rows
    is_mine = source == me_index
    run_start = jnp.sum((source < me_index).astype(jnp.int32), axis=1, keepdims=True)
    ranking = jnp.arange(CLUS, dtype=jnp.int32)[None, :]
    cluster_ids = jnp.arange(clusters, dtype=jnp.int32)[:, None]
    flat_slot = cluster_ids * capacity + ranking - run_start
    local_row = member_table - me_index * tok_rows
    slot_rows = (
        jnp.full((total,), tok_rows, jnp.int32)
        .at[jnp.where(is_mine, flat_slot, total).reshape(-1)]
        .set(local_row.reshape(-1), mode="drop")
    )
    home_slot = (
        jnp.zeros((tok_rows,), jnp.int32)
        .at[jnp.where(is_mine, local_row, tok_rows).reshape(-1)]
        .set(flat_slot.reshape(-1), mode="drop")
    )
    own_table = lax.dynamic_slice_in_dim(member_table, me_index * per_dev, per_dev, 0)
    own_source = own_table // tok_rows
    bins = jnp.arange(shards, dtype=jnp.int32)
    starts = jnp.sum((own_source[:, :, None] < bins[None, None, :]).astype(jnp.int32), axis=1)
    own_start = jnp.take_along_axis(starts, own_source, axis=1)
    local_ids = jnp.arange(per_dev, dtype=jnp.int32)[:, None]
    gather_index = ((own_source * per_dev + local_ids) * capacity + ranking - own_start).reshape(-1)
    causal = (jnp.arange(CLUS)[:, None] >= jnp.arange(CLUS)[None, :])[None]

    def outgoing(columns):
        return jnp.take(columns, slot_rows, axis=0, mode="fill", fill_value=0).reshape(
            shards, per_dev * capacity, -1
        )

    def packed(received):
        flat_rows = received.reshape(total, -1)
        return jnp.take(flat_rows, gather_index, axis=0).reshape(per_dev, CLUS, -1)

    def unpacked(results):
        res_width = results.shape[-1]
        spread = (
            jnp.zeros((total, res_width), results.dtype)
            .at[gather_index]
            .set(results.reshape(-1, res_width))
        )
        return spread.reshape(shards, per_dev * capacity, res_width)

    def delivered(returned):
        return jnp.take(returned.reshape(total, -1), home_slot, axis=0)

    route_query = query_rows[:, head_dim:]
    route_key = key_rows[:, head_dim:]
    route_value = value_rows[:, head_dim:]
    route_grad = out_grad[:, head_dim:]
    arrived = packed(
        lax.all_to_all(
            outgoing(jnp.concatenate([route_query, route_key, route_value], axis=1)),
            "seq",
            split_axis=0,
            concat_axis=0,
            tiled=True,
        )
    )
    group_query = arrived[:, :, :head_dim]
    group_key = arrived[:, :, head_dim : 2 * head_dim]
    group_value = arrived[:, :, 2 * head_dim :]
    forward_out = attend(group_query, group_key, group_value, None, causal, False)[0]
    route_out = delivered(
        lax.all_to_all(
            unpacked(forward_out.astype(jnp.bfloat16)),
            "seq",
            split_axis=0,
            concat_axis=0,
            tiled=True,
        )
    )
    group_grad = packed(
        lax.all_to_all(outgoing(route_grad), "seq", split_axis=0, concat_axis=0, tiled=True)
    )
    unused_out, query_gradient, key_gradient, value_gradient = attend(
        group_query, group_key, group_value, group_grad, causal, True
    )
    stacked = jnp.concatenate([query_gradient, key_gradient, value_gradient], axis=2).astype(
        jnp.bfloat16
    )
    route_grads = delivered(
        lax.all_to_all(unpacked(stacked), "seq", split_axis=0, concat_axis=0, tiled=True)
    )
    window_out, window_query, window_key, window_value = window_head(
        query_rows[:, :head_dim],
        key_rows[:, :head_dim],
        value_rows[:, :head_dim],
        out_grad[:, :head_dim],
    )
    attn_out = jnp.concatenate([window_out, route_out], axis=1)
    query_grad = jnp.concatenate([window_query, route_grads[:, :head_dim]], axis=1)
    key_grad = jnp.concatenate([window_key, route_grads[:, head_dim : 2 * head_dim]], axis=1)
    value_grad = jnp.concatenate([window_value, route_grads[:, 2 * head_dim :]], axis=1)
    return (attn_out, query_grad, key_grad, value_grad)


def solution(mesh):
    in_specs = (
        P("seq", "head"),
        P("seq", "head"),
        P("seq", "head"),
        P("seq", "head"),
        P(("seq", "head")),
    )
    out_specs = (P("seq", "head"), P("seq", "head"), P("seq", "head"), P("seq", "head"))
    return jax.shard_map(
        on_device, mesh=mesh, in_specs=in_specs, out_specs=out_specs, check_vma=False
    )
```

profile of v0, /device:TPU:32, one launch (start us, length us, event | category | flops | bytes accessed | tf_op | source)
XLA Modules:
  0.0 797.9 jit_solution(12446171369836373159)
XLA Ops:
  7.2 0.9 dynamic-update-slice.4
  8.1 0.6 copy-done.9
  8.8 455.9 %all-reduce.7.cloned.1.call-done = s32[16384]{0:T(1024)} async-done(((s32[16384]{0:T(1024)}), s32[16384]{0:T(1024)}) %all-reduce.7.cloned.1.call-update) | async-done | bytes 65552
  464.7 0.9 reshape.421
  465.8 0.9 compare_select_fusion
  466.7 60.3 %scatter_custom_fusion = s32[1024]{0:T(1024)S(1)} fusion(s32[16384]{0:T(1024)S(1)} %get-tuple-element.102, s32[16384]{0:T(1024)S(1)} %get-tuple-element.84, s32[]{:T(128)} %constant.170.clone.1), kind=kCustom, calls=%fused_computation.160 | custom fusion | bytes 4100 | tf_op jit(solution)/shard_map/scatter | solution.py:131
  527.1 3.2 gather_fusion.1
  530.4 0.9 broadcast_select_fusion.2
  531.3 7.1 all-to-all-start.2
  538.4 0.8 fusion.58
  539.2 13.0 %collective-permute-start.1 = (bf16[512,128]{1,0:T(8,128)(2,1)}, bf16[512,128]{1,0:T(8,128)(2,1)}, u32[]{:S(2)}, u32[]{:S(2)}) collective-permute-start(bf16[512,128]{1,0:T(8,128)(2,1)} %get-tuple-element.99), channel_id=1, source_target_pairs={{0,16},{16,32},{32,48},{48,64},{64,80},{80,96},{96,112},{112,128},... | collective-permute-start | bytes 393224 | tf_op jit(solution)/shard_map/ppermute | solution.py:15
  552.2 0.7 fusion.57
  552.9 2.7 collective-permute-start
  556.3 3.9 gather_fusion
  560.3 1.1 broadcast_select_fusion
  561.4 6.1 all-to-all-done.2
  567.4 10.3 %all-to-all-start = ((bf16[32,32,384]{2,1,0:T(8,128)(2,1)}), bf16[32,32,384]{2,1,0:T(8,128)(2,1)S(1)}, u32[]{:S(2)}, u32[]{:S(2)}) async-start(bf16[32,32,384]{2,1,0:T(8,128)(2,1)} %broadcast_select_fusion), calls=%async_computation | async-start | bytes 1572864 | tf_op jit(solution)/shard_map/all_to_all | solution.py:173
  577.8 60.3 %scatter_custom_fusion.2 = s32[512]{0:T(512)S(1)} fusion(s32[16384]{0:T(1024)S(1)} %get-tuple-element.83, s32[16384]{0:T(1024)S(1)} %bitcast.125, s32[]{:T(128)} %constant.177.clone.1), kind=kCustom, calls=%fused_computation.165 | custom fusion | bytes 2052 | tf_op jit(solution)/shard_map/scatter | solution.py:136
  638.2 0.7 fusion.60
  638.9 4.3 compare_select_fusion.5
  643.2 0.7 fusion.59
  644.1 15.4 %select_select_fusion = s32[512]{0:T(512)S(1)} fusion(pred[512]{0:T(512)(128)(4,1)S(1)} %get-tuple-element.81, pred[512]{0:T(512)(128)(4,1)S(1)} %get-tuple-element.80, pred[512]{0:T(512)(128)(4,1)S(1)} %get-tuple-element.82, pred[512]{0:T(512)(128)(4,1)S(1)} %get-tuple-element.79, pred[512]{0:T(512)(128)(4,1)S(1)} %get-tuple-element.78, ...), kind=kLoop, calls=%fused_computation.159 | loop fusion | flops 12800 | bytes 16996 | tf_op jit(solution)/shard_map/jit(take_along_axis)/gather | solution.py:142
  661.2 0.6 copy-done.20
  661.8 1.5 fusion.62
  664.4 3.3 fusion
  667.7 1.9 gather_fusion.4
  669.6 1.9 gather_fusion.2
  671.5 0.8 select_bitcast_fusion
  673.6 2.6 scatter_custom_fusion.1
  676.1 17.2 %all-to-all-start.1 = ((bf16[32,32,128]{2,1,0:T(8,128)(2,1)}), bf16[32,32,128]{2,1,0:T(8,128)(2,1)S(1)}, u32[]{:S(2)}, u32[]{:S(2)}) async-start(bf16[32,32,128]{2,1,0:T(8,128)(2,1)} %bitcast.51), calls=%async_computation.1 | async-start | bytes 524288 | tf_op jit(solution)/shard_map/all_to_all | solution.py:186
  693.4 1.7 multiply_reduce_fusion
  695.4 0.7 copy-done.4
  696.7 1.1 convolution_convert_fusion
  698.1 3.5 scatter_custom_fusion.3
  701.6 16.6 %all-to-all-done.1 = bf16[32,32,128]{2,1,0:T(8,128)(2,1)S(1)} async-done(((bf16[32,32,128]{2,1,0:T(8,128)(2,1)}), bf16[32,32,128]{2,1,0:T(8,128)(2,1)S(1)}, u32[]{:S(2)}, u32[]{:S(2)}) %all-to-all-start.1) | async-done | bytes 262176 | tf_op jit(solution)/shard_map/all_to_all | solution.py:186
  718.1 3.9 all-to-all-start.3
  722.1 2.2 fusion.3
  724.9 1.4 collective-permute-start.2
  726.9 1.4 collective-permute-start.3
  728.4 1.4 convolution_convert_fusion.5
  730.2 52.3 %collective-permute-done.2 = bf16[512,128]{0,1:T(8,128)(2,1)S(1)} collective-permute-done((bf16[512,128]{0,1:T(8,128)(2,1)S(1)}, bf16[512,128]{0,1:T(8,128)(2,1)S(1)}, u32[]{:S(2)}, u32[]{:S(2)}) %collective-permute-start.2) | collective-permute-done | bytes 131104 | tf_op jit(solution)/shard_map/ppermute | solution.py:15
  782.5 1.4 collective-permute-done.3
  783.9 1.3 gather_fusion.3
  785.4 0.8 copy.25
  786.3 1.9 gather_fusion.5
  788.5 0.8 copy.26
  789.4 0.8 copy.27
  790.2 0.8 copy.28
  (99 shorter events, 8.5 us)
Async XLA Ops:
  7.2 520.0 %slice-start = ((bf16[512,256]{1,0:T(8,128)(2,1)}), bf16[512,128]{1,0:T(8,128)(2,1)S(1)}, s32[]{:S(2)}) async-start(bf16[512,256]{1,0:T(8,128)(2,1)} %param.20), calls=%async_computation.5 | async-start | bytes 262144 | tf_op jit(solution)/shard_map/slice | solution.py:171
  7.2 457.5 %all-reduce.7.cloned.1.call-start = ((), (), s32[]{:S(2)}) async-start(), calls=%async_computation.4 | async-start | bytes 131072
  8.1 0.6 copy-start.9
  8.8 529.6 %copy-start.7 = (bf16[512,256]{1,0:T(8,128)(2,1)S(1)}, bf16[512,256]{1,0:T(8,128)(2,1)}, u32[]{:S(2)}) copy-start(bf16[512,256]{1,0:T(8,128)(2,1)} %param.19) | copy-start | bytes 786436
  466.7 85.5 %copy-start.8 = (bf16[512,256]{1,0:T(8,128)(2,1)S(1)}, bf16[512,256]{1,0:T(8,128)(2,1)}, u32[]{:S(2)}) copy-start(bf16[512,256]{1,0:T(8,128)(2,1)} %param.18) | copy-start | bytes 786436
  527.1 29.1 %slice-start.1 = ((bf16[512,256]{1,0:T(8,128)(2,1)}), bf16[512,128]{1,0:T(8,128)(2,1)S(1)}, s32[]{:S(2)}) async-start(bf16[512,256]{1,0:T(8,128)(2,1)} %param.17), calls=%async_computation.6 | async-start | bytes 262144 | tf_op jit(solution)/shard_map/slice | solution.py:168
  531.3 36.2 %all-to-all-start.2 = ((bf16[32,32,128]{2,1,0:T(8,128)(2,1)}), bf16[32,32,128]{2,1,0:T(8,128)(2,1)S(1)}, u32[]{:S(2)}, u32[]{:S(2)}) async-start(bf16[32,32,128]{2,1,0:T(8,128)(2,1)} %broadcast_select_fusion.2), calls=%async_computation.2 | async-start | bytes 524288 | tf_op jit(solution)/shard_map/all_to_all | solution.py:195
  539.2 124.6 %collective-permute-start.1 = (bf16[512,128]{1,0:T(8,128)(2,1)}, bf16[512,128]{1,0:T(8,128)(2,1)}, u32[]{:S(2)}, u32[]{:S(2)}) collective-permute-start(bf16[512,128]{1,0:T(8,128)(2,1)} %get-tuple-element.99), channel_id=1, source_target_pairs={{0,16},{16,32},{32,48},{48,64},{64,80},{80,96},{96,112},{112,128},... | collective-permute-start | bytes 393224 | tf_op jit(solution)/shard_map/ppermute | solution.py:15
  552.9 108.3 %collective-permute-start = (bf16[512,128]{1,0:T(8,128)(2,1)S(1)}, bf16[512,128]{1,0:T(8,128)(2,1)S(1)}, u32[]{:S(2)}, u32[]{:S(2)}) collective-permute-start(bf16[512,128]{1,0:T(8,128)(2,1)S(1)} %get-tuple-element.96), channel_id=1, source_target_pairs={{0,16},{16,32},{32,48},{48,64},{64,80},{80,96},{96,112},{112,128},... | collective-permute-start | bytes 393224 | tf_op jit(solution)/shard_map/ppermute | solution.py:15
  560.2 101.6 %copy-start.5 = (bf16[512,256]{1,0:T(8,128)(2,1)S(1)}, bf16[512,256]{1,0:T(8,128)(2,1)}, u32[]{:S(2)}) copy-start(bf16[512,256]{1,0:T(8,128)(2,1)} %param.17) | copy-start | bytes 786436
  560.2 101.6 %copy-start.12 = (bf16[1,512,128]{2,1,0:T(8,128)(2,1)S(1)}, bf16[1,512,128]{2,1,0:T(8,128)(2,1)}, u32[]{:S(2)}) copy-start(bf16[1,512,128]{2,1,0:T(8,128)(2,1)} %get-tuple-element.97) | copy-start | bytes 393220
  567.4 102.1 %all-to-all-start = ((bf16[32,32,384]{2,1,0:T(8,128)(2,1)}), bf16[32,32,384]{2,1,0:T(8,128)(2,1)S(1)}, u32[]{:S(2)}, u32[]{:S(2)}) async-start(bf16[32,32,384]{2,1,0:T(8,128)(2,1)} %broadcast_select_fusion), calls=%async_computation | async-start | bytes 1572864 | tf_op jit(solution)/shard_map/all_to_all | solution.py:173
  661.2 0.6 copy-start.20
  663.4 1.0 copy-start
  663.4 1.0 copy-start.10
  672.3 21.1 %copy-start.3 = (bf16[1,512,384]{2,1,0:T(8,128)(2,1)}, bf16[1,512,384]{2,1,0:T(8,128)(2,1)S(1)}, u32[]{:S(2)}) copy-start(bf16[1,512,384]{2,1,0:T(8,128)(2,1)S(1)} %select_bitcast_fusion) | copy-start | bytes 1179652
  672.6 1.0 copy-start.1
  672.8 22.3 %copy-start.15 = (f32[512]{0:T(512)}, f32[512]{0:T(512)S(1)}, u32[]{:S(2)}) copy-start(f32[512]{0:T(512)S(1)} %fusion.10) | copy-start | bytes 6148
  672.8 20.5 %copy-start.14 = (bf16[512,128]{1,0:T(8,128)(2,1)S(1)}, bf16[512,128]{1,0:T(8,128)(2,1)}, u32[]{:S(2)}) copy-start(bf16[512,128]{1,0:T(8,128)(2,1)} %gather_fusion.4) | copy-start | bytes 393220
  672.8 20.5 %copy-start.18 = (pred[512]{0:T(512)(128)(4,1)S(1)}, pred[512]{0:T(512)(128)(4,1)}, u32[]{:S(2)}) copy-start(pred[512]{0:T(512)(128)(4,1)} %compare_and_fusion.2) | copy-start | bytes 1540
  676.1 42.0 %all-to-all-start.1 = ((bf16[32,32,128]{2,1,0:T(8,128)(2,1)}), bf16[32,32,128]{2,1,0:T(8,128)(2,1)S(1)}, u32[]{:S(2)}, u32[]{:S(2)}) async-start(bf16[32,32,128]{2,1,0:T(8,128)(2,1)} %bitcast.51), calls=%async_computation.1 | async-start | bytes 524288 | tf_op jit(solution)/shard_map/all_to_all | solution.py:186
  693.4 1.8 copy-start.2
  695.1 1.0 copy-start.4
  695.1 1.6 copy-start.19
  697.8 24.2 %copy-start.17 = (f32[512]{0:T(512)S(1)}, f32[512]{0:T(512)}, u32[]{:S(2)}) copy-start(f32[512]{0:T(512)} %get-tuple-element.141) | copy-start | bytes 6148
  718.1 68.1 %all-to-all-start.3 = ((bf16[32,32,384]{2,1,0:T(8,128)(2,1)}), bf16[32,32,384]{2,1,0:T(8,128)(2,1)S(1)}, u32[]{:S(2)}, u32[]{:S(2)}) async-start(bf16[32,32,384]{2,1,0:T(8,128)(2,1)} %bitcast.122), calls=%async_computation.3 | async-start | bytes 1572864 | tf_op jit(solution)/shard_map/all_to_all | solution.py:204
  722.1 2.2 copy-start.6
  724.8 3.5 copy-start.11
  724.9 57.6 %collective-permute-start.2 = (bf16[512,128]{0,1:T(8,128)(2,1)S(1)}, bf16[512,128]{0,1:T(8,128)(2,1)S(1)}, u32[]{:S(2)}, u32[]{:S(2)}) collective-permute-start(bf16[512,128]{0,1:T(8,128)(2,1)S(1)} %fusion.22), channel_id=1, source_target_pairs={{16,0},{32,16},{48,32},{64,48},{80,64},{96,80},{112,96},{128,112},... | collective-permute-start | bytes 393224 | tf_op jit(solution)/shard_map/ppermute | solution.py:15
  726.9 2.9 copy-start.13
  726.9 2.9 copy-start.21
  726.9 56.9 %collective-permute-start.3 = (bf16[512,128]{0,1:T(8,128)(2,1)S(1)}, bf16[512,128]{0,1:T(8,128)(2,1)S(1)}, u32[]{:S(2)}, u32[]{:S(2)}) collective-permute-start(bf16[512,128]{0,1:T(8,128)(2,1)S(1)} %fusion.21), channel_id=1, source_target_pairs={{16,0},{32,16},{48,32},{64,48},{80,64},{96,80},{112,96},{128,112},... | collective-permute-start | bytes 393224 | tf_op jit(solution)/shard_map/ppermute | solution.py:15
  729.8 55.5 %copy-start.16 = (pred[512]{0:T(512)(128)(4,1)S(1)}, pred[512]{0:T(512)(128)(4,1)}, u32[]{:S(2)}) copy-start(pred[512]{0:T(512)(128)(4,1)} %compare_and_fusion.1) | copy-start | bytes 1540
Sparse Core Ops, SparseCore 0:
  14.0 450.6 all-reduce.6
where the time goes:
time: 799 us; the launch traced here: 798 us
  waiting for transfers between devices  532 us (67%)
  local copies, waits for them, and re-layouts  153 us (19%)
  starting transfers between devices  57.2 us (7%)
  other arithmetic  29.5 us (4%)
  between operations  14.7 us (2%)
  matrix products  11.7 us (1%)
    unnamed x2, waiting for transfers between devices  456 us
    scatter x1, local copies, waits for them, and re-layouts, on_device(): slot_rows = jnp.full((total,), tok_rows, jnp.int32).at[jnp.where(is_mine,...  60.3 us
    scatter x1, local copies, waits for them, and re-layouts, on_device(): home_slot = jnp.zeros((tok_rows,), jnp.int32).at[jnp.where(is_mine, local...  60.3 us
    ppermute x4, waiting for transfers between devices, from_behind(): return lax.ppermute(array, axis, pairs)  53.6 us
    gather x3, other arithmetic, on_device(): own_start = jnp.take_along_axis(starts, own_source, axis=1)  19.8 us
    ppermute x4, starting transfers between devices, from_behind(): return lax.ppermute(array, axis, pairs)  18.6 us
    all_to_all x1, starting transfers between devices, on_device(): lax.all_to_all(unpacked(forward_out.astype(jnp.bfloat16)), 'seq', split_a...  17.2 us
    all_to_all x1, waiting for transfers between devices, on_device(): lax.all_to_all(unpacked(forward_out.astype(jnp.bfloat16)), 'seq', split_a...  16.6 us
  transfers between devices with their start and end apart: 9, of which 5 were waited for; matrix products, arithmetic and copies ran while one was open for 14% of the time, Pallas kernels for 0%

commit v1 on v0

v1 whole, which is shorter than its diff:
```python
import math

import jax
import jax.numpy as jnp
from jax import lax
from jax.experimental import pallas as pl
from jax.experimental.pallas import tpu as pltpu
from jax.sharding import Mesh
from jax.sharding import PartitionSpec as P

HD = 128
TOK = 512
CAP = 32
NX, NY, NZH, NZL, NCORE = 4, 4, 2, 8, 2
NPLANE = NX * NY * NCORE
NCOL = NZH * NZL
SLOTS = NPLANE * CAP
AXES = ("x", "y", "zh", "zl", "core")
MESH = pl.DeviceIdType.MESH
F32 = jnp.float32
BF16 = jnp.bfloat16
SCALE = 1.0 / math.sqrt(HD)


def iota(shape, dim):
    return lax.broadcasted_iota(jnp.int32, shape, dim)


def iotaf(shape, dim):
    return iota(shape, dim).astype(F32)


def dot_nn(a, b):
    return lax.dot_general(a, b, (((1,), (0,)), ((), ())), preferred_element_type=F32)


def dot_nt(a, b):
    return lax.dot_general(a, b, (((1,), (1,)), ((), ())), preferred_element_type=F32)


def dot_tn(a, b):
    return lax.dot_general(a, b, (((0,), (0,)), ((), ())), preferred_element_type=F32)


def attend_rows(query, grad, parts):
    scores = [jnp.where(mask, dot_nt(key, query) * SCALE, -jnp.inf) for key, _, mask in parts]
    top = None
    for score in scores:
        part_top = jnp.max(score, axis=0, keepdims=True)
        top = part_top if top is None else jnp.maximum(top, part_top)
    terms = [jnp.exp(score - top) for score in scores]
    total = sum(jnp.sum(term, axis=0, keepdims=True) for term in terms)
    inverse = 1.0 / total
    probs = [term * inverse for term in terms]
    weights = [prob.astype(BF16) for prob in probs]
    grad_probs = [dot_nt(value, grad) for _, value, _ in parts]
    delta = sum(
        jnp.sum(prob * grad_prob, axis=0, keepdims=True)
        for prob, grad_prob in zip(probs, grad_probs)
    )
    grad_scores = [
        (prob * (grad_prob - delta) * SCALE).astype(BF16)
        for prob, grad_prob in zip(probs, grad_probs)
    ]
    out = sum(dot_tn(value, weight) for (_, value, _), weight in zip(parts, weights))
    grad_query = sum(dot_tn(key, gs) for (key, _, _), gs in zip(parts, grad_scores))
    return out.T, grad_query.T, weights, grad_scores, (top, inverse, delta)


def kernel(
    q_ref, k_ref, v_ref, g_ref, mem_ref,
    o_ref, dq_ref, dk_ref, dv_ref,
    piece, colbuf, tile, planebuf, lists,
    xbuf, rim, stat_out, stat_in,
    pack, pack_t, sort, sort_t,
    sbuf, rbuf, xc, res, sbuf2, rbuf2, bsend, brecv,
    col_s, col_r, plane_s, plane_r, swap_s, swap_r, rim_s, rim_r, stat_s, stat_r,
    fwd_s, fwd_r, bwd_s, bwd_r, back_s, back_r,
):
    x, y, zh, zl, core = [lax.axis_index(a) for a in AXES]
    z = zh * NZL + zl
    i = x * NY + y
    p = core * (NX * NY) + i
    seq = i * 2 + zh

    def in_plane(index):
        spot = lax.rem(index, NX * NY)
        return (spot // NY, lax.rem(spot, NY), zh, zl, index // (NX * NY))

    def in_column(depth):
        return (x, y, depth // NZL, lax.rem(depth, NZL), core)

    def of_seq(index):
        spot = index // 2
        return (spot // NY, lax.rem(spot, NY), lax.rem(index, 2), zl, core)

    swap_dev = (x, y, 1 - zh, zl, 1 - core)
    next_dev = of_seq(lax.rem(seq + 1, 32))
    prev_dev = of_seq(lax.rem(seq + 31, 32))
    far_dev = of_seq(lax.rem(seq + 31 + 2 * zh, 32))
    swapped = zh != core

    def remote(src, dst, send, recv, device):
        return pltpu.make_async_remote_copy(
            src_ref=src, dst_ref=dst, send_sem=send, recv_sem=recv,
            device_id=device, device_id_type=MESH,
        )

    def wait_bytes(ref, sem):
        pltpu.make_async_copy(ref, ref, sem).wait()

    h = zl * 2 + core
    lane_part = iota((1, 128), 1) // 32
    stat_out[...] = jnp.zeros_like(stat_out)
    piece[0] = jnp.where(lane_part == lax.rem(h, 4), mem_ref[...], 0)

    barrier = pltpu.get_barrier_semaphore()

    def greet(device):
        pl.semaphore_signal(barrier, inc=1, device_id=device, device_id_type=MESH)

    @pl.loop(1, NCOL)
    def _(d):
        greet(in_column(lax.rem(z + d, NCOL)))

    @pl.loop(1, NPLANE)
    def _(d):
        greet(in_plane(lax.rem(p + d, NPLANE)))

    greet(far_dev)
    greet(swap_dev)
    pl.semaphore_wait(barrier, NCOL - 1 + NPLANE - 1 + 2)

    @pl.loop(1, NCOL)
    def _(d):
        remote(
            piece.at[0], colbuf.at[z], col_s, col_r, in_column(lax.rem(z + d, NCOL))
        ).start()

    inputs = (q_ref, k_ref, v_ref, g_ref)
    route = pl.ds(HD, HD)
    local = pl.ds(0, HD)
    swaps = [
        remote(
            inputs[t].at[:, route],
            xbuf.at[t // 2, :, pl.ds((t % 2) * HD, HD)],
            swap_s.at[t], swap_r.at[t], swap_dev,
        )
        for t in range(4)
    ]
    rims = [
        remote(ref.at[:, local], rim.at[t], rim_s.at[t], rim_r.at[t], device)
        for t, (ref, device) in enumerate(
            ((k_ref, next_dev), (v_ref, next_dev), (q_ref, prev_dev), (g_ref, prev_dev))
        )
    ]

    @pl.when(swapped)
    def _():
        for copy in swaps:
            copy.start()
        for copy in rims:
            copy.start()

    @pl.when(jnp.logical_not(swapped))
    def _():
        for t in range(4):
            xbuf[t // 2, :, (t % 2) * HD : (t % 2 + 1) * HD] = inputs[t][:, HD:]

    colbuf[pl.ds(z, 1)] = piece[...]
    wait_bytes(colbuf.at[pl.ds(0, NCOL - 1)], col_r)
    for row in range(8):
        first = (row // 4) * NZL + (row % 4) * 2
        tile[row : row + 1, :] = colbuf[first] + colbuf[first + 1]

    @pl.loop(1, NPLANE)
    def _(d):
        remote(
            tile, planebuf.at[p], plane_s, plane_r, in_plane(lax.rem(p + d, NPLANE))
        ).start()

    planebuf[pl.ds(p, 1)] = tile[...][None]
    wait_bytes(planebuf.at[pl.ds(0, NPLANE - 1)], plane_r)
    for row in range(8):
        rows = planebuf[0:16, row, :] + planebuf[16:32, row, :]
        half, group = row // 4, row % 4
        lists[half * 16 : half * 16 + 16, group * 128 : (group + 1) * 128] = rows.astype(F32)

    base = ((2 * i + core) * TOK).astype(F32)

    @pl.loop(0, 8)
    def _(group):
        token_row = jnp.zeros((1, 128), F32)
        for member in range(4):
            cluster = group * 4 + member
            row = lists[pl.ds(cluster, 1), :]
            start = jnp.sum(jnp.where(row < base, 1.0, 0.0), axis=1, keepdims=True)
            wanted = iotaf((CAP, TOK), 0) + start
            picked = jnp.where(iotaf((CAP, TOK), 1) == wanted, row + 1.0, 0.0)
            token = jnp.sum(picked, axis=1, keepdims=True) - (1.0 + base)
            onehot = jnp.where(iotaf((CAP, TOK), 1) == token, 1.0, 0.0)
            pack[pl.ds(pl.multiple_of(cluster * CAP, CAP), CAP), :] = onehot.astype(BF16)
            placed = iota((CAP, 128), 1) == iota((CAP, 128), 0) + CAP * member
            token_row += jnp.sum(jnp.where(placed, token, 0.0), axis=0, keepdims=True)
        onehot = jnp.where(iotaf((TOK, 128), 0) == token_row, 1.0, 0.0)
        pack_t[:, pl.ds(pl.multiple_of(group * 128, 128), 128)] = onehot.astype(BF16)

    own = lists[pl.ds(p, 1), :].astype(jnp.int32)
    block = own >> 9
    same = iota((NPLANE, TOK), 0) == block
    earlier = jnp.sum(
        jnp.where(block < iota((NPLANE, TOK), 0), 1.0, 0.0), axis=1, keepdims=True
    )
    run_start = jnp.sum(jnp.where(same, earlier, 0.0), axis=0, keepdims=True)
    source = ((block & 1) * 16 + (block >> 1)) * CAP
    slot_row = source.astype(F32) + iotaf((1, TOK), 1) - run_start
    for part in range(8):
        rows = iotaf((128, TOK), 0) + part * 128.0
        sort_t[part * 128 : (part + 1) * 128, :] = jnp.where(rows == slot_row, 1.0, 0.0).astype(BF16)
    for part in range(4):
        piece_row = slot_row[:, part * 128 : (part + 1) * 128]
        diagonal = iota((128, 128), 0) == iota((128, 128), 1)
        slot_col = jnp.sum(jnp.where(diagonal, piece_row, 0.0), axis=1, keepdims=True)
        onehot = jnp.where(iotaf((128, SLOTS), 1) == slot_col, 1.0, 0.0)
        sort[part * 128 : (part + 1) * 128, :] = onehot.astype(BF16)

    @pl.when(jnp.logical_not(swapped))
    def _():
        for copy in rims:
            copy.start()

    def exchange(from_buf, to_buf, g, send, recv):
        @pl.loop(1, NPLANE)
        def _(d):
            other = lax.rem(p + d, NPLANE)
            remote(
                from_buf.at[g, other], to_buf.at[g, p], send.at[g], recv.at[g], in_plane(other)
            ).start()

        to_buf[g, pl.ds(p, 1)] = from_buf[g, pl.ds(p, 1)]

    def fill(to_buf, g, matrix, data):
        for part in range(4):
            rows = dot_nn(matrix[part * 256 : (part + 1) * 256, :], data)
            to_buf[g, part * 8 : (part + 1) * 8] = rows.astype(BF16).reshape(8, CAP, 2 * HD)

    for g in range(2):

        @pl.when(swapped)
        def _():
            swaps[2 * g].wait_recv()
            swaps[2 * g + 1].wait_recv()

        fill(sbuf, g, pack, xbuf[g])
        exchange(sbuf, rbuf, g, fwd_s, fwd_r)

    for g in range(2):
        wait_bytes(rbuf.at[g, pl.ds(0, NPLANE - 1)], fwd_r.at[g])
        xc[g] = dot_nn(sort[...], rbuf[g].reshape(SLOTS, 2 * HD)).astype(BF16)

    half = TOK // 2

    def cluster_rows(qb):
        lo = qb * half
        nk = lo + half
        query = xc[0, lo : lo + half, :HD]
        grad = xc[1, lo : lo + half, HD:]
        key = xc[0, :nk, HD:]
        value = xc[1, :nk, :HD]
        mask = iota((nk, half), 0) <= iota((nk, half), 1) + lo
        out, grad_query, weights, grad_scores, _ = attend_rows(query, grad, [(key, value, mask)])
        res[0, lo : lo + half, :HD] = out.astype(BF16)
        res[0, lo : lo + half, HD:] = grad_query.astype(BF16)
        return dot_nn(grad_scores[0], query), dot_nn(weights[0], grad)

    dk_a, dv_a = cluster_rows(0)
    dk_b, dv_b = cluster_rows(1)
    fill(sbuf2, 0, sort_t, res[0])
    exchange(sbuf2, rbuf2, 0, bwd_s, bwd_r)
    res[1, :half, :HD] = (dk_a + dk_b[:half]).astype(BF16)
    res[1, half:, :HD] = dk_b[half:].astype(BF16)
    res[1, :half, HD:] = (dv_a + dv_b[:half]).astype(BF16)
    res[1, half:, HD:] = dv_b[half:].astype(BF16)
    fill(sbuf2, 1, sort_t, res[1])
    exchange(sbuf2, rbuf2, 1, bwd_s, bwd_r)

    rims[0].wait_recv()
    rims[1].wait_recv()
    hide = jnp.where(seq == 0, 4 * TOK, 0)
    own_parts = []
    for qb in range(2):
        lo = qb * half
        nk = lo + half
        query = q_ref[lo : lo + half, :HD]
        grad = g_ref[lo : lo + half, :HD]
        behind = TOK - lo
        rim_mask = iota((behind, half), 0) + lo > iota((behind, half), 1) + lo + hide
        own_mask = iota((nk, half), 0) <= iota((nk, half), 1) + lo
        out, grad_query, weights, grad_scores, stats = attend_rows(
            query,
            grad,
            [
                (rim[0, lo:, :], rim[1, lo:, :], rim_mask),
                (k_ref[:nk, :HD], v_ref[:nk, :HD], own_mask),
            ],
        )
        o_ref[lo : lo + half, :HD] = out.astype(BF16)
        dq_ref[lo : lo + half, :HD] = grad_query.astype(BF16)
        for row, stat in enumerate(stats):
            stat_out[row : row + 1, lo : lo + half] = stat
        own_parts.append((dot_nn(grad_scores[1], query), dot_nn(weights[1], grad)))
    stats_copy = remote(stat_out, stat_in, stat_s, stat_r, prev_dev)
    stats_copy.start()

    targets = ((o_ref, dq_ref), (dk_ref, dv_ref))
    backs = [
        remote(bsend.at[g], brecv.at[g], back_s.at[g], back_r.at[g], swap_dev) for g in range(2)
    ]
    for g in range(2):
        wait_bytes(rbuf2.at[g, pl.ds(0, NPLANE - 1)], bwd_r.at[g])
        bsend[g] = dot_nn(pack_t[...], rbuf2[g].reshape(SLOTS, 2 * HD)).astype(BF16)

        @pl.when(swapped)
        def _():
            backs[g].start()

        @pl.when(jnp.logical_not(swapped))
        def _():
            targets[g][0][:, HD:] = bsend[g, :, :HD]
            targets[g][1][:, HD:] = bsend[g, :, HD:]

    rims[2].wait_recv()
    rims[3].wait_recv()
    stats_copy.wait_recv()
    last = jnp.where(seq == 31, 4 * TOK, 0)
    next_parts = []
    for qb in range(2):
        lo = qb * half
        behind = TOK - lo
        query = rim[2, lo : lo + half, :]
        grad = rim[3, lo : lo + half, :]
        key = k_ref[lo:, :HD]
        value = v_ref[lo:, :HD]
        mask = iota((behind, half), 0) > iota((behind, half), 1) + last
        score = jnp.where(mask, dot_nt(key, query) * SCALE, -jnp.inf)
        top, inverse, delta = [stat_in[row : row + 1, lo : lo + half] for row in range(3)]
        prob = jnp.exp(score - top) * inverse
        weight = prob.astype(BF16)
        grad_score = (prob * (dot_nt(value, grad) - delta) * SCALE).astype(BF16)
        next_parts.append((dot_nn(grad_score, query), dot_nn(weight, grad)))
    for t, ref in enumerate((dk_ref, dv_ref)):
        own_a, own_b = own_parts[0][t], own_parts[1][t]
        next_a, next_b = next_parts[0][t], next_parts[1][t]
        ref[:half, :HD] = (own_a + own_b[:half] + next_a[:half]).astype(BF16)
        ref[half:, :HD] = (own_b[half:] + next_a[half:] + next_b).astype(BF16)

    @pl.when(swapped)
    def _():
        for g in range(2):
            backs[g].wait_recv()
            targets[g][0][:, HD:] = brecv[g, :, :HD]
            targets[g][1][:, HD:] = brecv[g, :, HD:]
        for copy in swaps:
            copy.wait_send()
        for copy in backs:
            copy.wait_send()

    for copy in rims:
        copy.wait_send()
    stats_copy.wait_send()
    wait_bytes(colbuf.at[pl.ds(0, NCOL - 1)], col_s)
    wait_bytes(planebuf.at[pl.ds(0, NPLANE - 1)], plane_s)
    for g in range(2):
        wait_bytes(rbuf.at[g, pl.ds(0, NPLANE - 1)], fwd_s.at[g])
        wait_bytes(rbuf2.at[g, pl.ds(0, NPLANE - 1)], bwd_s.at[g])


def on_device(query_rows, key_rows, value_rows, out_grad, members):
    vmem = pl.BlockSpec(memory_space=pltpu.VMEM)
    shape = jax.ShapeDtypeStruct((TOK, 2 * HD), BF16)
    padded = pltpu.VMEM((2, NPLANE, CAP, 2 * HD), BF16)
    pair = pltpu.VMEM((2, TOK, 2 * HD), BF16)
    dma = pltpu.SemaphoreType.DMA
    return pl.pallas_call(
        kernel,
        out_shape=(shape,) * 4,
        in_specs=[vmem] * 5,
        out_specs=(vmem,) * 4,
        scratch_shapes=[
            pltpu.VMEM((1, 1, 128), jnp.int32),
            pltpu.VMEM((NCOL, 1, 128), jnp.int32),
            pltpu.VMEM((8, 128), jnp.int32),
            pltpu.VMEM((NPLANE, 8, 128), jnp.int32),
            pltpu.VMEM((NPLANE, TOK), F32),
            pair,
            pltpu.VMEM((4, TOK, HD), BF16),
            pltpu.VMEM((8, TOK), F32),
            pltpu.VMEM((8, TOK), F32),
            pltpu.VMEM((SLOTS, TOK), BF16),
            pltpu.VMEM((TOK, SLOTS), BF16),
            pltpu.VMEM((TOK, SLOTS), BF16),
            pltpu.VMEM((SLOTS, TOK), BF16),
            padded, padded, pair, pair, padded, padded, pair, pair,
            dma, dma, dma, dma, dma((4,)), dma((4,)), dma((4,)), dma((4,)), dma, dma,
            dma((2,)), dma((2,)), dma((2,)), dma((2,)), dma((2,)), dma((2,)),
        ],
        compiler_params=pltpu.CompilerParams(collective_id=0, has_side_effects=True),
    )(query_rows, key_rows, value_rows, out_grad, jnp.tile(members, 4).reshape(1, 128))


def solution(mesh):
    fine = Mesh(mesh.devices.reshape(NX, NY, NZH, NZL, NCORE), AXES)
    rows, cols = ("x", "y", "zh"), ("zl", "core")
    spec = P(rows, cols)
    return jax.shard_map(
        on_device,
        mesh=fine,
        in_specs=(spec, spec, spec, spec, P(AXES)),
        out_specs=(spec,) * 4,
        check_vma=False,
    )
```

time: 799 us -> 134 us (0.17)
  the two profiles are of different devices: /device:TPU:32 before, /device:TPU:89 now
where the time goes in v1:
time: 134 us
  Pallas kernels  127 us (95%)
  local copies, waits for them, and re-layouts  5.76 us (4%)
    pallas_call x1, Pallas kernels, on_device(): pl.pallas_call(kernel, out_shape=(shape,) * 4, in_specs=[vmem] * 5, out_s...  127 us
    unnamed x10, local copies, waits for them, and re-layouts  4.5 us

profile of v1, /device:TPU:89, one launch (start us, length us, event | category | flops | bytes accessed | tf_op | source)
XLA Modules:
  0.0 133.9 jit_solution(11656676331960223703)
XLA Ops:
  0.6 0.7 tile.2
  1.3 0.6 reshape_tile.3.mem_ref
  1.9 127.5 %shard_map.84 = (bf16[512,256]{1,0:T(8,128)(2,1)}, bf16[512,256]{1,0:T(8,128)(2,1)}, bf16[512,256]{1,0:T(8,128)(2,1)}, bf16[512,256]{1,0:T(8,128)(2,1)}) custom-call(bf16[512,256]{1,0:T(8,128)(2,1)} %q_ref.1, bf16[512,256]{1,0:T(8,128)(2,1)} %k_ref.1, bf16[512,256]{1,0:T(8,128)(2,1)} %v_ref.1, bf16[512,256]{1,0:T(8,128)(2,1)} %g_ref.1, ...), custom_call_target="tpu_custom_call" | custom-call | tf_op jit(solution)/shard_map/pallas_call | solution.py:384
  129.4 0.0 copy-start.2
  129.4 1.7 %copy.13 = bf16[512,256]{1,0:T(8,128)(2,1)} copy(bf16[512,256]{1,0:T(8,128)(2,1)} %get-tuple-element.8) | data formatting | bytes 524288
  131.1 0.0 copy-done.2
  131.1 0.0 copy-start.1
  131.1 0.7 copy.14
  131.8 0.3 copy-done.1
  132.2 0.0 copy-start
  132.2 0.7 copy.15
  132.9 0.3 copy-done
  133.2 0.7 copy.16
Async XLA Ops:
  129.4 1.7 %copy-start.2 = (bf16[512,256]{1,0:T(8,128)(2,1)S(1)}, bf16[512,256]{1,0:T(8,128)(2,1)}, u32[]{:S(2)}) copy-start(bf16[512,256]{1,0:T(8,128)(2,1)} %get-tuple-element.9) | copy-start | bytes 786436
  131.1 1.0 copy-start.1
  132.2 1.0 copy-start

commit v2 on v1

--- a/solution.py
+++ b/solution.py
@@ -110,14 +110,22 @@
         pltpu.make_async_copy(ref, ref, sem).wait()
 
     h = zl * 2 + core
-    lane_part = iota((1, 128), 1) // 32
     stat_out[...] = jnp.zeros_like(stat_out)
-    piece[0] = jnp.where(lane_part == lax.rem(h, 4), mem_ref[...], 0)
+    piece[0] = jnp.zeros((1, 128), jnp.int32)
+    for quarter in range(4):
+
+        @pl.when(lax.rem(h, 4) == quarter)
+        def _():
+            piece[0, :, quarter * 32 : quarter * 32 + 32] = mem_ref[...]
+
 
     barrier = pltpu.get_barrier_semaphore()
 
     def greet(device):
         pl.semaphore_signal(barrier, inc=1, device_id=device, device_id_type=MESH)
+
+    greet(swap_dev)
+    greet(far_dev)
 
     @pl.loop(1, NCOL)
     def _(d):
@@ -127,8 +135,6 @@
     def _(d):
         greet(in_plane(lax.rem(p + d, NPLANE)))
 
-    greet(far_dev)
-    greet(swap_dev)
     pl.semaphore_wait(barrier, NCOL - 1 + NPLANE - 1 + 2)
 
     @pl.loop(1, NCOL)
@@ -158,8 +164,6 @@
     @pl.when(swapped)
     def _():
         for copy in swaps:
-            copy.start()
-        for copy in rims:
             copy.start()
 
     @pl.when(jnp.logical_not(swapped))
@@ -224,10 +228,6 @@
         onehot = jnp.where(iotaf((128, SLOTS), 1) == slot_col, 1.0, 0.0)
         sort[part * 128 : (part + 1) * 128, :] = onehot.astype(BF16)
 
-    @pl.when(jnp.logical_not(swapped))
-    def _():
-        for copy in rims:
-            copy.start()
 
     def exchange(from_buf, to_buf, g, send, recv):
         @pl.loop(1, NPLANE)
@@ -253,6 +253,8 @@
 
         fill(sbuf, g, pack, xbuf[g])
         exchange(sbuf, rbuf, g, fwd_s, fwd_r)
+    for copy in rims:
+        copy.start()
 
     for g in range(2):
         wait_bytes(rbuf.at[g, pl.ds(0, NPLANE - 1)], fwd_r.at[g])
@@ -375,13 +377,18 @@
         wait_bytes(rbuf2.at[g, pl.ds(0, NPLANE - 1)], bwd_s.at[g])
 
 
+def write_out(*refs):
+    for src, dst in zip(refs[:4], refs[4:]):
+        dst[...] = src[...]
+
+
 def on_device(query_rows, key_rows, value_rows, out_grad, members):
     vmem = pl.BlockSpec(memory_space=pltpu.VMEM)
     shape = jax.ShapeDtypeStruct((TOK, 2 * HD), BF16)
     padded = pltpu.VMEM((2, NPLANE, CAP, 2 * HD), BF16)
     pair = pltpu.VMEM((2, TOK, 2 * HD), BF16)
     dma = pltpu.SemaphoreType.DMA
-    return pl.pallas_call(
+    results = pl.pallas_call(
         kernel,
         out_shape=(shape,) * 4,
         in_specs=[vmem] * 5,
@@ -405,7 +412,15 @@
             dma((2,)), dma((2,)), dma((2,)), dma((2,)), dma((2,)), dma((2,)),
         ],
         compiler_params=pltpu.CompilerParams(collective_id=0, has_side_effects=True),
-    )(query_rows, key_rows, value_rows, out_grad, jnp.tile(members, 4).reshape(1, 128))
+    )(query_rows, key_rows, value_rows, out_grad, members.reshape(1, 32))
+
+
+    return pl.pallas_call(
+        write_out,
+        out_shape=(shape,) * 4,
+        in_specs=[vmem] * 4,
+        out_specs=(vmem,) * 4,
+    )(*results)
 
 
 def solution(mesh):

time: 134 us -> 125 us (0.933)
  the two profiles are of different devices: /device:TPU:89 before, /device:TPU:43 now
where the time goes in v2:
time: 125 us
  Pallas kernels  124 us (99%)
    pallas_call x1, Pallas kernels, on_device(): pl.pallas_call(kernel, out_shape=(shape,) * 4, in_specs=[vmem] * 5, out_s...  122 us

profile of v2, /device:TPU:43, one launch (start us, length us, event | category | flops | bytes accessed | tf_op | source)
XLA Modules:
  0.0 124.6 jit_solution(3215278006139106984)
XLA Ops:
  0.6 121.8 %shard_map.84 = (bf16[512,256]{1,0:T(8,128)(2,1)}, bf16[512,256]{1,0:T(8,128)(2,1)}, bf16[512,256]{1,0:T(8,128)(2,1)}, bf16[512,256]{1,0:T(8,128)(2,1)}) custom-call(bf16[512,256]{1,0:T(8,128)(2,1)} %q_ref.1, bf16[512,256]{1,0:T(8,128)(2,1)} %k_ref.1, bf16[512,256]{1,0:T(8,128)(2,1)} %v_ref.1, bf16[512,256]{1,0:T(8,128)(2,1)} %g_ref.1, s32[1,32]{1,0:T(1,128)} %bitcast.1), custom_call_target="tpu_custom_call" | custom-call | tf_op jit(solution)/shard_map/pallas_call | solution.py:391
  122.4 2.2 %shard_map.85 = (bf16[512,256]{1,0:T(8,128)(2,1)}, bf16[512,256]{1,0:T(8,128)(2,1)}, bf16[512,256]{1,0:T(8,128)(2,1)}, bf16[512,256]{1,0:T(8,128)(2,1)}) custom-call(bf16[512,256]{1,0:T(8,128)(2,1)} %get-tuple-element.8.refs_0_, bf16[512,256]{1,0:T(8,128)(2,1)} %get-tuple-element.9.refs_1_, bf16[512,256]{1,0:T(8,128)(2,1)} %get-tuple-element.10.refs_2_, ...), custom_call_target="tpu_custom_call" | custom-call | tf_op jit(solution)/shard_map/pallas_call | solution.py:418

commit v3 on v2

--- a/solution.py
+++ b/solution.py
@@ -68,8 +68,9 @@
 
 
 def kernel(
-    q_ref, k_ref, v_ref, g_ref, mem_ref,
+    q_hbm, k_hbm, v_hbm, g_hbm, mem_ref,
     o_ref, dq_ref, dk_ref, dv_ref,
+    q_ref, k_ref, v_ref, g_ref, load_s,
     piece, colbuf, tile, planebuf, lists,
     xbuf, rim, stat_out, stat_in,
     pack, pack_t, sort, sort_t,
@@ -110,6 +111,15 @@
         pltpu.make_async_copy(ref, ref, sem).wait()
 
     h = zl * 2 + core
+    loads = [
+        pltpu.make_async_copy(src, dst, load_s.at[t])
+        for t, (src, dst) in enumerate(
+            ((q_hbm, q_ref), (k_hbm, k_ref), (v_hbm, v_ref), (g_hbm, g_ref))
+        )
+    ]
+    for load in loads:
+        load.start()
+
     stat_out[...] = jnp.zeros_like(stat_out)
     piece[0] = jnp.zeros((1, 128), jnp.int32)
     for quarter in range(4):
@@ -142,6 +152,9 @@
         remote(
             piece.at[0], colbuf.at[z], col_s, col_r, in_column(lax.rem(z + d, NCOL))
         ).start()
+
+    for load in loads:
+        load.wait()
 
     inputs = (q_ref, k_ref, v_ref, g_ref)
     route = pl.ds(HD, HD)
@@ -384,6 +397,8 @@
 
 def on_device(query_rows, key_rows, value_rows, out_grad, members):
     vmem = pl.BlockSpec(memory_space=pltpu.VMEM)
+    hbm = pl.BlockSpec(memory_space=pltpu.HBM)
+    block = pltpu.VMEM((TOK, 2 * HD), BF16)
     shape = jax.ShapeDtypeStruct((TOK, 2 * HD), BF16)
     padded = pltpu.VMEM((2, NPLANE, CAP, 2 * HD), BF16)
     pair = pltpu.VMEM((2, TOK, 2 * HD), BF16)
@@ -391,9 +406,10 @@
     results = pl.pallas_call(
         kernel,
         out_shape=(shape,) * 4,
-        in_specs=[vmem] * 5,
+        in_specs=[hbm] * 4 + [vmem],
         out_specs=(vmem,) * 4,
         scratch_shapes=[
+            block, block, block, block, pltpu.SemaphoreType.DMA((4,)),
             pltpu.VMEM((1, 1, 128), jnp.int32),
             pltpu.VMEM((NCOL, 1, 128), jnp.int32),
             pltpu.VMEM((8, 128), jnp.int32),
@@ -411,8 +427,16 @@
             dma, dma, dma, dma, dma((4,)), dma((4,)), dma((4,)), dma((4,)), dma, dma,
             dma((2,)), dma((2,)), dma((2,)), dma((2,)), dma((2,)), dma((2,)),
         ],
-        compiler_params=pltpu.CompilerParams(collective_id=0, has_side_effects=True),
-    )(query_rows, key_rows, value_rows, out_grad, members.reshape(1, 32))
+        compiler_params=pltpu.CompilerParams(
+            collective_id=0, has_side_effects=True, vmem_limit_bytes=24 * 2**20
+        ),
+    )(
+        *[
+            pltpu.with_memory_space_constraint(rows, pltpu.HBM)
+            for rows in (query_rows, key_rows, value_rows, out_grad)
+        ],
+        pltpu.with_memory_space_constraint(members.reshape(1, 32), pltpu.HBM),
+    )
 
 
     return pl.pallas_call(
@@ -420,6 +444,7 @@
         out_shape=(shape,) * 4,
         in_specs=[vmem] * 4,
         out_specs=(vmem,) * 4,
+        compiler_params=pltpu.CompilerParams(vmem_limit_bytes=8 * 2**20),
     )(*results)
 
 

time: 125 us -> 123 us (0.984)
  the two profiles are of different devices: /device:TPU:43 before, /device:TPU:77 now
where the time goes in v3:
time: 123 us
  Pallas kernels  122 us (99%)
    pallas_call x1, Pallas kernels, on_device(): pl.pallas_call(kernel, out_shape=(shape,) * 4, in_specs=[hbm] * 4 + [vmem...  121 us

profile of v3, /device:TPU:77, one launch (start us, length us, event | category | flops | bytes accessed | tf_op | source)
XLA Modules:
  0.0 122.6 jit_solution(17212985481320997302)
XLA Ops:
  0.6 121.0 %shard_map.84 = (bf16[512,256]{1,0:T(8,128)(2,1)S(1)}, bf16[512,256]{1,0:T(8,128)(2,1)S(1)}, bf16[512,256]{1,0:T(8,128)(2,1)S(1)}, bf16[512,256]{1,0:T(8,128)(2,1)S(1)}) custom-call(bf16[512,256]{1,0:T(8,128)(2,1)} %q_hbm.1, bf16[512,256]{1,0:T(8,128)(2,1)} %k_hbm.1, bf16[512,256]{1,0:T(8,128)(2,1)} %v_hbm.1, bf16[512,256]{1,0:T(8,128)(2,1)} %g_hbm.1, ...), custom_call_target="tpu_custom_call" | custom-call | tf_op jit(solution)/shard_map/pallas_call | solution.py:406
  121.6 1.0 shard_map.85

commit v4 on v3

--- a/solution.py
+++ b/solution.py
@@ -298,6 +298,26 @@
     res[1, half:, HD:] = dv_b[half:].astype(BF16)
     fill(sbuf2, 1, sort_t, res[1])
     exchange(sbuf2, rbuf2, 1, bwd_s, bwd_r)
+
+    targets = ((o_ref, dq_ref), (dk_ref, dv_ref))
+    backs = [
+        remote(bsend.at[g], brecv.at[g], back_s.at[g], back_r.at[g], swap_dev) for g in range(2)
+    ]
+
+    def give_back(g):
+        wait_bytes(rbuf2.at[g, pl.ds(0, NPLANE - 1)], bwd_r.at[g])
+        bsend[g] = dot_nn(pack_t[...], rbuf2[g].reshape(SLOTS, 2 * HD)).astype(BF16)
+
+        @pl.when(swapped)
+        def _():
+            backs[g].start()
+
+        @pl.when(jnp.logical_not(swapped))
+        def _():
+            targets[g][0][:, HD:] = bsend[g, :, :HD]
+            targets[g][1][:, HD:] = bsend[g, :, HD:]
+
+    give_back(0)
 
     rims[0].wait_recv()
     rims[1].wait_recv()
@@ -327,22 +347,7 @@
     stats_copy = remote(stat_out, stat_in, stat_s, stat_r, prev_dev)
     stats_copy.start()
 
-    targets = ((o_ref, dq_ref), (dk_ref, dv_ref))
-    backs = [
-        remote(bsend.at[g], brecv.at[g], back_s.at[g], back_r.at[g], swap_dev) for g in range(2)
-    ]
-    for g in range(2):
-        wait_bytes(rbuf2.at[g, pl.ds(0, NPLANE - 1)], bwd_r.at[g])
-        bsend[g] = dot_nn(pack_t[...], rbuf2[g].reshape(SLOTS, 2 * HD)).astype(BF16)
-
-        @pl.when(swapped)
-        def _():
-            backs[g].start()
-
-        @pl.when(jnp.logical_not(swapped))
-        def _():
-            targets[g][0][:, HD:] = bsend[g, :, :HD]
-            targets[g][1][:, HD:] = bsend[g, :, HD:]
+    give_back(1)
 
     rims[2].wait_recv()
     rims[3].wait_recv()

time: 123 us -> 124 us (level)
  no operation moved by 1% of the time
where the time goes in v4:
time: 124 us
  Pallas kernels  123 us (99%)
    pallas_call x1, Pallas kernels, on_device(): pl.pallas_call(kernel, out_shape=(shape,) * 4, in_specs=[hbm] * 4 + [vmem...  122 us

profile of v4, /device:TPU:77, one launch (start us, length us, event | category | flops | bytes accessed | tf_op | source)
XLA Modules:
  0.0 123.8 jit_solution(8468630343379770935)
XLA Ops:
  0.6 122.2 %shard_map.84 = (bf16[512,256]{1,0:T(8,128)(2,1)S(1)}, bf16[512,256]{1,0:T(8,128)(2,1)S(1)}, bf16[512,256]{1,0:T(8,128)(2,1)S(1)}, bf16[512,256]{1,0:T(8,128)(2,1)S(1)}) custom-call(bf16[512,256]{1,0:T(8,128)(2,1)} %q_hbm.1, bf16[512,256]{1,0:T(8,128)(2,1)} %k_hbm.1, bf16[512,256]{1,0:T(8,128)(2,1)} %v_hbm.1, bf16[512,256]{1,0:T(8,128)(2,1)} %g_hbm.1, ...), custom_call_target="tpu_custom_call" | custom-call | tf_op jit(solution)/shard_map/pallas_call | solution.py:411
  122.8 1.0 shard_map.85
